TPU v7x, 128 devices: a whole 4x4x4 slice. The times are simulated.
128 devices in a mesh: half: 2 (over core), grp: 64 (over x, y, z).
Axes of the slice: x: 4, y: 4, z: 4, core: 2. Of those that a mesh axis runs over, the one named last changes fastest.
Arguments:
- weights: float32 [2, 64, 2, 8192, 128], P('half', 'grp'), may hold values from -4 to 4
- accum: float32 [2, 64, 2, 8192], P('half', 'grp'), may hold values from 0.01 to 1
- grads: float32 [128, 128, 16, 128], P(('half', 'grp')), may hold values from -24 to 24
- row_ids: int32 [128, 128, 16], P(('half', 'grp')), may hold values from 0 to 16383
- counts: int32 [128, 128], P(('half', 'grp')), may hold values from 1 to 16, as said below
Outputs:
- new_weights: float32 [2, 64, 2, 8192, 128], P('half', 'grp')
- new_accum: float32 [2, 64, 2, 8192], P('half', 'grp')
Inputs may be any that keep to these rules, and one draw needn't show every extreme that they name: `counts`: A few owners, the same for all senders, receive 16 live rows from every sender; no two of them share a shard index g (owners g and 64 + g). The owner that shares its shard index with such an owner receives 16 // 2 live rows from every sender; each other count lies from 1 to 8. So the two owners of one shard index receive at most 24 live rows from one sender together, and some pair receives exactly that.
All inputs are finite; a program needn't handle non-finite values.
Results may differ from a plain program's by a relative error of at most 0.00002.
Values sent between devices are 32-bit elements; how exact they have to be, the bound alone decides.
No kernel may reach another device: no remote copies, remote signals or barrier semaphores. Data moves between devices by JAX's collectives and lax.ppermute only.
A program may use at most 128 MiB of HBM per device.

v0:
```python
import jax
import jax.numpy as jnp
from jax import lax
from jax.sharding import PartitionSpec as P

LEARN_RATE = 0.5
EPSILON = 1e-06


def partner(value, axis, stride):
    mask = 2**stride
    pairs = [(source, source ^ mask) for source in range(lax.axis_size(axis))]
    return lax.ppermute(value, axis, pairs)


def per_device(weights, accum, grads, row_ids, counts):
    owners = grads.shape[1]
    slots = grads.shape[2]
    width = grads.shape[3]
    rows_half = weights.shape[3]
    top_bit = lax.axis_index("half")
    table = weights[0, 0]
    state = accum[0, 0]
    kept = lax.dynamic_index_in_dim(table, top_bit, 0, keepdims=False)
    given = lax.dynamic_index_in_dim(table, 1 - top_bit, 0, keepdims=False)
    kept_acc = lax.dynamic_index_in_dim(state, top_bit, 0, keepdims=False)
    given_acc = lax.dynamic_index_in_dim(state, 1 - top_bit, 0, keepdims=False)
    gotten, gotten_acc = partner((given, given_acc), "half", 0)
    slot_index = lax.broadcasted_iota(jnp.int32, (owners, slots), 1)
    live = slot_index < counts[0][:, None]
    masked = jnp.where(live[..., None], grads[0], jnp.zeros_like(grads[0]))
    ids_local = row_ids[0]
    received, got_ids = (
        lax.all_to_all(masked, ("half", "grp"), split_axis=0, concat_axis=0, tiled=True),
        lax.all_to_all(ids_local, ("half", "grp"), split_axis=0, concat_axis=0, tiled=True),
    )
    total = (
        jnp.zeros((2 * rows_half, width), jnp.float32)
        .at[got_ids.reshape(-1)]
        .add(received.reshape(-1, width))
    )
    is_low = top_bit == 0
    moved = jnp.where(
        is_low, jnp.concatenate([kept, gotten], 0), jnp.concatenate([gotten, kept], 0)
    )
    moved_acc = jnp.where(
        is_low,
        jnp.concatenate([kept_acc, gotten_acc], 0),
        jnp.concatenate([gotten_acc, kept_acc], 0),
    )
    accumulated = moved_acc + jnp.mean(total * total, axis=-1)
    updated = moved - LEARN_RATE * total / (jnp.sqrt(accumulated)[:, None] + EPSILON)
    return (updated.reshape(1, 1, 2, rows_half, width), accumulated.reshape(1, 1, 2, rows_half))


def solution(mesh):
    placed = (
        P("half", "grp", None, None, None),
        P("half", "grp", None, None),
        P(("half", "grp"), None, None, None),
        P(("half", "grp"), None, None),
        P(("half", "grp"), None),
    )
    return jax.shard_map(
        per_device,
        mesh=mesh,
        in_specs=placed,
        out_specs=(P("half", "grp", None, None, None), P("half", "grp", None, None)),
        check_vma=False,
    )
```

profile of v0, /device:TPU:0, one launch (start us, length us, event | category | flops | bytes accessed | tf_op | source)
XLA Modules:
  0.0 85.2 jit_solution(9578131386032756872)
XLA Ops:
  0.6 0.0 copy-start.2
  0.6 0.0 copy-start.3
  0.7 0.0 copy-start
  0.7 0.0 copy-start.1
  0.7 7.3 %dynamic-slice_bitcast_fusion.1 = (f32[8192,128]{1,0:T(8,128)}, f32[8192,128]{1,0:T(8,128)}) fusion(f32[1,1,2,8192,128]{4,3,2,1,0:T(8,128)} %param.5, s32[]{:T(128)S(6)} %select_n.53, s32[]{:T(128)S(6)} %select_n.54), kind=kLoop, calls=%fused_computation.7 | loop fusion | bytes 16777224 | tf_op jit(solution)/shard_map/jit(dynamic_index_in_dim)/squeeze | solution.py:24
  8.0 0.0 collective-permute-start
  8.0 0.7 copy.8
  8.7 11.3 %all-to-all-start = ((s32[128,1,16]{2,1,0:T(1,128)}), s32[128,1,16]{2,1,0:T(1,128)S(1)}, u32[]{:S(2)}, u32[]{:S(2)}) async-start(s32[128,1,16]{2,1,0:T(1,128)} %bitcast.2), calls=%async_computation | async-start | bytes 131072 | tf_op jit(solution)/shard_map/all_to_all | solution.py:35
  20.0 0.1 iota_compare_fusion
  20.1 1.3 %bitcast_select_fusion = f32[128,16,128]{2,1,0:T(8,128)} fusion(f32[1,128,16,128]{3,2,1,0:T(8,128)S(1)} %copy-done, pred[128,16]{1,0:T(8,128)(4,1)S(1)} %iota_compare_fusion), kind=kLoop, calls=%fused_computation.8 | loop fusion | flops 262144 | bytes 2099200 | tf_op jit(solution)/shard_map/jit(_where)/select_n | solution.py:31
  21.4 7.5 %all-to-all-done = s32[128,1,16]{2,1,0:T(1,128)S(1)} async-done(((s32[128,1,16]{2,1,0:T(1,128)}), s32[128,1,16]{2,1,0:T(1,128)S(1)}, u32[]{:S(2)}, u32[]{:S(2)}) %all-to-all-start) | async-done | bytes 8224 | tf_op jit(solution)/shard_map/all_to_all | solution.py:35
  29.0 5.0 %all-to-all-start.1 = ((f32[128,16,128]{2,1,0:T(8,128)}), f32[128,16,128]{2,1,0:T(8,128)S(1)}, u32[]{:S(2)}, u32[]{:S(2)}) async-start(f32[128,16,128]{2,1,0:T(8,128)} %bitcast_select_fusion), calls=%async_computation.1 | async-start | bytes 2097152 | tf_op jit(solution)/shard_map/all_to_all | solution.py:34
  34.0 0.1 constant_dynamic-slice_fusion
  34.0 0.1 collective-permute-start.1
  34.1 0.5 broadcast.60
  34.6 0.8 reduce.3
  35.5 0.1 reshape.149
  35.6 16.5 %all-to-all-done.1 = f32[128,16,128]{2,1,0:T(8,128)S(1)} async-done(((f32[128,16,128]{2,1,0:T(8,128)}), f32[128,16,128]{2,1,0:T(8,128)S(1)}, u32[]{:S(2)}, u32[]{:S(2)}) %all-to-all-start.1) | async-done | bytes 1048608 | tf_op jit(solution)/shard_map/all_to_all | solution.py:34
  52.0 15.3 %scatter_custom_fusion = f32[16384,128]{1,0:T(8,128)} fusion(s32[2048]{0:T(1024)S(1)} %bitcast.17, f32[2048,128]{1,0:T(8,128)S(1)} %bitcast.14, f32[]{:T(128)} %constant.38.clone.1), kind=kCustom, calls=%fused_computation.4 | custom fusion | flops 262144 | bytes 8388612 | tf_op jit(solution)/shard_map/scatter-add | solution.py:40
  67.4 4.6 %multiply_reduce_fusion = f32[16384]{0:T(1024)S(1)} fusion(f32[16384,128]{1,0:T(8,128)} %scatter_custom_fusion), kind=kLoop, calls=%fused_computation.3 | loop fusion | flops 4177920 | bytes 8454144 | tf_op jit(solution)/shard_map/reduce_sum | solution.py:51
  72.0 0.0 collective-permute-done.1
  72.1 0.7 add.61
  72.7 0.0 collective-permute-done
  72.7 12.5 %fusion = f32[16384,128]{1,0:T(8,128)} fusion(f32[8192,128]{1,0:T(8,128)} %collective-permute-done, f32[8192,128]{1,0:T(8,128)} %get-tuple-element.4, f32[16384,128]{1,0:T(8,128)} %scatter_custom_fusion, f32[16384]{0:T(1024)S(1)} %get-tuple-element.2, pred[]{:T(512)S(6)} %eq.3), kind=kLoop, calls=%fused_computation.2 | loop fusion | flops 12582912 | bytes 25231360 | tf_op jit(solution)/shard_map/sub | solution.py:52
  (6 shorter events, 0.1 us)
Async XLA Ops:
  0.6 7.3 %copy-start.2 = (s32[1,128,16]{1,2,0:T(8,128)S(1)}, s32[1,128,16]{1,2,0:T(8,128)}, u32[]{:S(2)}) copy-start(s32[1,128,16]{1,2,0:T(8,128)} %param.8) | copy-start | bytes 24580
  0.6 19.4 %copy-start.3 = (s32[1,128]{1,0:T(1,128)S(1)}, s32[1,128]{1,0:T(1,128)}, u32[]{:S(2)}) copy-start(s32[1,128]{1,0:T(1,128)} %param.9) | copy-start | bytes 1540
  0.7 19.4 %copy-start = (f32[1,128,16,128]{3,2,1,0:T(8,128)S(1)}, f32[1,128,16,128]{3,2,1,0:T(8,128)}, u32[]{:S(2)}) copy-start(f32[1,128,16,128]{3,2,1,0:T(8,128)} %param.7) | copy-start | bytes 3145732
  0.7 33.3 %copy-start.1 = (f32[1,1,2,8192]{3,2,1,0:T(2,128)S(1)}, f32[1,1,2,8192]{3,2,1,0:T(2,128)}, u32[]{:S(2)}) copy-start(f32[1,1,2,8192]{3,2,1,0:T(2,128)} %param.6) | copy-start | bytes 196612
  8.0 64.8 %collective-permute-start = (f32[8192,128]{1,0:T(8,128)}, f32[8192,128]{1,0:T(8,128)}, u32[]{:S(2)}, u32[]{:S(2)}) collective-permute-start(f32[8192,128]{1,0:T(8,128)} %get-tuple-element.5), channel_id=1, source_target_pairs={{0,64},{64,0},{1,65},{65,1},{2,66},{66,2},{3,67},{67,3},{4,68},{68... | collective-permute-start | bytes 12582920 | tf_op jit(solution)/shard_map/ppermute | solution.py:13
  8.7 20.2 %all-to-all-start = ((s32[128,1,16]{2,1,0:T(1,128)}), s32[128,1,16]{2,1,0:T(1,128)S(1)}, u32[]{:S(2)}, u32[]{:S(2)}) async-start(s32[128,1,16]{2,1,0:T(1,128)} %bitcast.2), calls=%async_computation | async-start | bytes 131072 | tf_op jit(solution)/shard_map/all_to_all | solution.py:35
  29.0 23.1 %all-to-all-start.1 = ((f32[128,16,128]{2,1,0:T(8,128)}), f32[128,16,128]{2,1,0:T(8,128)S(1)}, u32[]{:S(2)}, u32[]{:S(2)}) async-start(f32[128,16,128]{2,1,0:T(8,128)} %bitcast_select_fusion), calls=%async_computation.1 | async-start | bytes 2097152 | tf_op jit(solution)/shard_map/all_to_all | solution.py:34
  34.0 38.0 %collective-permute-start.1 = (f32[8192]{0:T(1024)S(1)}, f32[8192]{0:T(1024)S(1)}, u32[]{:S(2)}, u32[]{:S(2)}) collective-permute-start(f32[8192]{0:T(1024)S(1)} %bitcast.16), channel_id=1, source_target_pairs={{0,64},{64,0},{1,65},{65,1},{2,66},{66,2},{3,67},{67,3},{4,68},{68... | collective-permute-start | bytes 98312 | tf_op jit(solution)/shard_map/ppermute | solution.py:13
where the time goes:
time: 85.5 us; the launch traced here: 85.2 us
  other arithmetic  34.7 us (41%)
  waiting for transfers between devices  24 us (28%)
  starting transfers between devices  16.4 us (19%)
  local copies, waits for them, and re-layouts  9.38 us (11%)
    all_to_all x1, waiting for transfers between devices, per_device(): lax.all_to_all(masked, ('half', 'grp'), split_axis=0, concat_axis=0, tile...  16.5 us
    scatter-add x1, other arithmetic, per_device(): total = jnp.zeros((2 * rows_half, width), jnp.float32).at[got_ids.reshape...  15.3 us
    sub x1, other arithmetic, per_device(): moved - LEARN_RATE * total / (jnp.sqrt(accumulated)[:, None] + EPSILON)  12.5 us
    all_to_all x1, starting transfers between devices, per_device(): lax.all_to_all(ids_local, ('half', 'grp'), split_axis=0, concat_axis=0, t...  11.3 us
    all_to_all x1, waiting for transfers between devices, per_device(): lax.all_to_all(ids_local, ('half', 'grp'), split_axis=0, concat_axis=0, t...  7.53 us
    squeeze x1, local copies, waits for them, and re-layouts, per_device(): kept = lax.dynamic_index_in_dim(table, top_bit, 0, keepdims=False)  7.3 us
    all_to_all x1, starting transfers between devices, per_device(): lax.all_to_all(masked, ('half', 'grp'), split_axis=0, concat_axis=0, tile...  4.99 us
    reduce_sum x1, other arithmetic, per_device(): accumulated = moved_acc + jnp.mean(total * total, axis=-1)  4.62 us
  transfers between devices with their start and end apart: 4, of which 2 were waited for; matrix products, arithmetic and copies ran while one was open for 28% of the time, Pallas kernels for 0%

commit v1 on v0

v1 whole, which is shorter than its diff:
```python
import functools

import jax
import jax.numpy as jnp
from jax import lax
from jax.experimental import pallas as pl
from jax.experimental.pallas import tpu as pltpu
from jax.sharding import PartitionSpec as P

LEARN_RATE = 0.5
EPSILON = 1e-06
BLOCK = 128
CHUNK = 1024
BANKS = 2


def pack_kernel(slots, dead, grads_ref, ids_ref, counts_ref, out_ref):
    owners = ids_ref.shape[1]
    stride = slots + 1
    slot = lax.broadcasted_iota(jnp.int32, ids_ref.shape, 0)
    marked = jnp.where(slot < counts_ref[...], ids_ref[...], dead).astype(jnp.float32)
    filler = jnp.zeros((BLOCK - slots, owners), jnp.float32)
    out_ref[pl.ds(slots, owners, stride=stride), :] = jnp.concatenate([marked, filler], 0).T
    for owner in range(owners):
        out_ref[stride * owner : stride * owner + slots, :] = grads_ref[
            slots * owner : slots * (owner + 1), :
        ]


def pack(grads, ids, counts, dead):
    owners, slots, width = grads.shape
    vmem = pl.BlockSpec(memory_space=pltpu.VMEM)
    return pl.pallas_call(
        functools.partial(pack_kernel, slots, dead),
        out_shape=jax.ShapeDtypeStruct((owners * (slots + 1), width), jnp.float32),
        in_specs=[vmem] * 3,
        out_specs=vmem,
        name="pack",
    )(grads.reshape(owners * slots, width), ids.T, counts)


def update_kernel(
    slots,
    bit_ref,
    own_ref,
    got_ref,
    own_acc_ref,
    got_acc_ref,
    rows_ref,
    out_ref,
    out_acc_ref,
    table,
    *scratch,
):
    banks = scratch[:BANKS]
    ids_v, ids_s, in_sem, out_sem, ids_sem = scratch[BANKS:]
    bit = bit_ref[0]
    half_rows = own_ref.shape[1]
    width = own_ref.shape[2]
    senders = rows_ref.shape[0] // (slots + 1)
    stride = slots + 1
    per_half = half_rows // CHUNK

    def fetch(src, chunk):
        return pltpu.make_async_copy(
            src.at[bit, pl.ds((chunk % per_half) * CHUNK, CHUNK), :],
            table.at[pl.ds(chunk * CHUNK, CHUNK), :],
            in_sem.at[chunk],
        )

    wide = rows_ref[pl.ds(slots, senders, stride=stride), :].T
    ids_v[...] = wide[:slots, :].astype(jnp.int32)
    to_scalar = pltpu.make_async_copy(ids_v, ids_s, ids_sem)
    to_scalar.start()
    for top in range(2):
        for chunk in range(top * per_half, (top + 1) * per_half):

            @pl.when(bit == top)
            def _():
                fetch(own_ref, chunk).start()

            @pl.when(bit != top)
            def _():
                fetch(got_ref, chunk).start()

    zero = jnp.zeros((256, width), jnp.float32)

    def clear(step, carry):
        for bank in banks:
            bank[pl.ds(pl.multiple_of(step * 256, 256), 256), :] = zero
        return carry

    lax.fori_loop(0, 2 * half_rows // 256, clear, 0)
    to_scalar.wait()

    def gather(sender, carry):
        base = sender * stride
        for slot in range(slots):
            row = ids_s[slot, sender]
            bank = banks[slot % BANKS]
            bank[pl.ds(row, 1), :] = bank[pl.ds(row, 1), :] + rows_ref[pl.ds(base + slot, 1), :]
        return carry

    lax.fori_loop(0, senders, gather, 0)

    ones = jnp.ones((8, width), jnp.bfloat16)
    contract = (((1,), (1,)), ((), ()))

    def flush(chunk):
        return pltpu.make_async_copy(
            table.at[pl.ds(chunk * CHUNK, CHUNK), :],
            out_ref.at[pl.ds(chunk * CHUNK, CHUNK), :],
            out_sem.at[chunk],
        )

    for top in range(2):

        def finish(step, carry, top=top):
            chunk = top * per_half + step
            fetch(own_ref, chunk).wait()
            for block in range(CHUNK // BLOCK):
                start = pl.multiple_of(chunk * CHUNK + block * BLOCK, BLOCK)
                at = pl.ds(start, BLOCK)
                lanes = pl.ds(pl.multiple_of(step * CHUNK + block * BLOCK, BLOCK), BLOCK)
                total = banks[0][at, :]
                for bank in banks[1:]:
                    total = total + bank[at, :]
                square = total * total
                high = square.astype(jnp.bfloat16)
                low = (square - high.astype(jnp.float32)).astype(jnp.bfloat16)
                summed = lax.dot_general(
                    ones, high, contract, preferred_element_type=jnp.float32
                ) + lax.dot_general(ones, low, contract, preferred_element_type=jnp.float32)
                own = own_acc_ref[:, lanes]
                got = got_acc_ref[:, lanes]
                pair = jnp.where(bit == top, own, got)
                state = jnp.where(bit == 0, pair[0:1, :], pair[1:2, :])
                state = state + summed[0:1, :] * (1.0 / width)
                out_acc_ref[pl.ds(top, 1), lanes] = state
                scale = LEARN_RATE / (jnp.sqrt(state) + EPSILON)
                scale = jnp.broadcast_to(scale, (BLOCK, BLOCK)).T
                table[at, :] = table[at, :] - total * scale
            flush(chunk).start()
            return carry

        lax.fori_loop(0, per_half, finish, 0)

    for chunk in range(2 * per_half):
        flush(chunk).wait()


def update(bit, own, got, own_acc, got_acc, rows, slots):
    halves, half_rows, width = own.shape
    senders = rows.shape[0] // (slots + 1)
    chunks = halves * half_rows // CHUNK
    vmem = pl.BlockSpec(memory_space=pltpu.VMEM)
    hbm = pl.BlockSpec(memory_space=pltpu.HBM)
    smem = pl.BlockSpec(memory_space=pltpu.SMEM)
    return pl.pallas_call(
        functools.partial(update_kernel, slots),
        out_shape=(
            jax.ShapeDtypeStruct((halves * half_rows, width), jnp.float32),
            jax.ShapeDtypeStruct((halves, half_rows), jnp.float32),
        ),
        in_specs=[smem, hbm, hbm, vmem, vmem, vmem],
        out_specs=(hbm, vmem),
        scratch_shapes=[
            pltpu.VMEM((halves * half_rows, width), jnp.float32),
            *[pltpu.VMEM((halves * half_rows + 8, width), jnp.float32) for _ in range(BANKS)],
            pltpu.VMEM((slots, senders), jnp.int32),
            pltpu.SMEM((slots, senders), jnp.int32),
            pltpu.SemaphoreType.DMA((chunks,)),
            pltpu.SemaphoreType.DMA((chunks,)),
            pltpu.SemaphoreType.DMA,
        ],
        compiler_params=pltpu.CompilerParams(vmem_limit_bytes=60 * 1024 * 1024),
        name="update",
    )(bit, own, got, own_acc, got_acc, rows)


def per_device(weights, accum, grads, row_ids, counts):
    owners, slots, width = grads.shape[1:]
    halves, half_rows = weights.shape[2:4]
    swap = [(0, 1), (1, 0)]
    table = weights[0, 0]
    state = accum[0, 0]
    got = lax.ppermute(table, "half", swap)
    got_acc = lax.ppermute(state, "half", swap)
    packed = pack(grads[0], row_ids[0], counts, halves * half_rows)
    rows = lax.all_to_all(
        packed.reshape(owners, 1, (slots + 1) * width),
        ("half", "grp"),
        split_axis=0,
        concat_axis=0,
        tiled=True,
    ).reshape(owners * (slots + 1), width)
    bit = lax.axis_index("half").astype(jnp.int32).reshape(1)
    new_weights, new_accum = update(bit, table, got, state, got_acc, rows, slots)
    return (
        new_weights.reshape(1, 1, halves, half_rows, width),
        new_accum.reshape(1, 1, halves, half_rows),
    )


def solution(mesh):
    placed = (
        P("half", "grp", None, None, None),
        P("half", "grp", None, None),
        P(("half", "grp"), None, None, None),
        P(("half", "grp"), None, None),
        P(("half", "grp"), None),
    )
    return jax.shard_map(
        per_device,
        mesh=mesh,
        in_specs=placed,
        out_specs=(P("half", "grp", None, None, None), P("half", "grp", None, None)),
        check_vma=False,
    )
```

time: 85.5 us -> 53.3 us (0.62)
  other arithmetic: 34.7 us -> 0 us
  Pallas kernels: 0 us -> 21.2 us
  local copies, waits for them, and re-layouts: 9.38 us -> 1.08 us
  waiting for transfers between devices: 24 us -> 18.7 us
  starting transfers between devices: 16.4 us -> 11.4 us
    pallas_call x0 -> x2, Pallas kernels: none -> 21.2 us  [the longest x1 18.9 us: update(): pl.pallas_call(functools.partial(update_kernel, slots), out_shape=(jax.Sh...]
    scatter-add x1 -> x0, other arithmetic: 15.3 us -> none  [per_device(): total = jnp.zeros((2 * rows_half, width), jnp.float32).at[got_ids.reshape...]
    sub x1 -> x0, other arithmetic: 12.5 us -> none  [per_device(): moved - LEARN_RATE * total / (jnp.sqrt(accumulated)[:, None] + EPSILON)]
    squeeze x1 -> x0, local copies, waits for them, and re-layouts: 7.3 us -> none  [per_device(): kept = lax.dynamic_index_in_dim(table, top_bit, 0, keepdims=False)]
    all_to_all x2 -> x1, waiting for transfers between devices: 24 us -> 17.2 us  [per_device(): lax.all_to_all(packed.reshape(owners, 1, (slots + 1) * width), ('half', '...]
    all_to_all x2 -> x1, starting transfers between devices: 16.3 us -> 11.3 us  [per_device(): lax.all_to_all(packed.reshape(owners, 1, (slots + 1) * width), ('half', '...]
    reduce_sum x1 -> x0, other arithmetic: 4.62 us -> none  [per_device(): accumulated = moved_acc + jnp.mean(total * total, axis=-1)]
    ppermute x2, waiting for transfers between devices: 0.01 us -> 1.45 us  [the longest x1 1.45 us: per_device(): got_acc = lax.ppermute(state, 'half', swap)]
  transfers between devices with their start and end apart: 4 -> 3, of which waited for: 2 -> 2; matrix products, arithmetic and copies ran while one was open for 28% -> 0% of each run, Pallas kernels for 0% -> 4%
where the time goes in v1:
time: 53.3 us; the launch traced here: 53.1 us
  Pallas kernels  21.2 us (40%)
  waiting for transfers between devices  18.7 us (35%)
  starting transfers between devices  11.4 us (21%)
  local copies, waits for them, and re-layouts  1.08 us (2%)
  between operations  0.67 us (1%)
    pallas_call x1, Pallas kernels, update(): pl.pallas_call(functools.partial(update_kernel, slots), out_shape=(jax.Sh...  18.9 us
    all_to_all x1, waiting for transfers between devices, per_device(): lax.all_to_all(packed.reshape(owners, 1, (slots + 1) * width), ('half', '...  17.2 us
    all_to_all x1, starting transfers between devices, per_device(): lax.all_to_all(packed.reshape(owners, 1, (slots + 1) * width), ('half', '...  11.3 us
    pallas_call x1, Pallas kernels, pack(): pl.pallas_call(functools.partial(pack_kernel, slots, dead), out_shape=jax...  2.34 us
    ppermute x1, waiting for transfers between devices, per_device(): got_acc = lax.ppermute(state, 'half', swap)  1.45 us
    unnamed x4, local copies, waits for them, and re-layouts  1.08 us
  transfers between devices with their start and end apart: 3, of which 2 were waited for; matrix products, arithmetic and copies ran while one was open for 0% of the time, Pallas kernels for 4%

profile of v1, /device:TPU:0, one launch (start us, length us, event | category | flops | bytes accessed | tf_op | source)
XLA Modules:
  0.0 53.1 jit_solution(1469621910810561359)
XLA Ops:
  0.6 0.1 collective-permute-start
  0.7 2.3 %pack.1 = f32[2176,128]{1,0:T(8,128)} custom-call(f32[2048,128]{1,0:T(8,128)} %bitcast.15, s32[16,128]{1,0:T(8,128)} %bitcast.18, s32[1,128]{1,0:T(1,128)} %counts_ref.1), custom_call_target="tpu_custom_call" | custom-call | tf_op jit(solution)/shard_map/pack/pallas_call | solution.py:33
  3.1 11.3 %all-to-all-start = ((f32[128,1,2176]{2,1,0:T(1,128)}), f32[128,1,2176]{2,1,0:T(1,128)S(1)}, u32[]{:S(2)}, u32[]{:S(2)}) async-start(f32[128,1,2176]{2,1,0:T(1,128)} %bitcast.13), calls=%async_computation | async-start | bytes 2228224 | tf_op jit(solution)/shard_map/all_to_all | solution.py:190
  14.3 0.1 collective-permute-start.1
  14.4 1.4 %collective-permute-done.1.got_acc_ref = f32[2,8192]{1,0:T(2,128)S(1)} collective-permute-done((f32[2,8192]{1,0:T(2,128)}, f32[2,8192]{1,0:T(2,128)S(1)}, u32[]{:S(2)}, u32[]{:S(2)}) %collective-permute-start.1) | collective-permute-done | bytes 65568 | tf_op jit(solution)/shard_map/ppermute | solution.py:188
  15.9 0.0 copy-start.1
  15.9 17.2 %all-to-all-done = f32[128,1,2176]{2,1,0:T(1,128)S(1)} async-done(((f32[128,1,2176]{2,1,0:T(1,128)}), f32[128,1,2176]{2,1,0:T(1,128)S(1)}, u32[]{:S(2)}, u32[]{:S(2)}) %all-to-all-start) | async-done | bytes 1114144 | tf_op jit(solution)/shard_map/all_to_all | solution.py:190
  33.1 0.0 copy-start
  33.1 0.0 collective-permute-done.got_ref
  33.1 0.0 copy-done.1
  33.1 1.1 %copy-done = f32[128,1,2176]{2,1,0:T(1,128)} copy-done((f32[128,1,2176]{2,1,0:T(1,128)}, f32[128,1,2176]{2,1,0:T(1,128)S(1)}, u32[]{:S(2)}) %copy-start) | copy-done | bytes 1114136
  34.2 18.9 %update.1 = (f32[16384,128]{1,0:T(8,128)}, f32[2,8192]{1,0:T(2,128)}) custom-call(s32[1]{0:T(128)} %bitcast.bit_ref, f32[2,8192,128]{2,1,0:T(8,128)} %bitcast.12, f32[2,8192,128]{2,1,0:T(8,128)} %collective-permute-done.got_ref, f32[2,8192]{1,0:T(2,128)} %bitcast.17, f32[2,8192]{1,0:T(2,128)} %copy-done.1, f32[2176,128]{1,0:T(8,128)} %bitcast.14), custom_call_target="tpu_custom_call" | custom-call | tf_op jit(solution)/shard_map/update/pallas_call | solution.py:159
Async XLA Ops:
  0.6 32.5 %collective-permute-start = (f32[2,8192,128]{2,1,0:T(8,128)}, f32[2,8192,128]{2,1,0:T(8,128)}, u32[]{:S(2)}, u32[]{:S(2)}) collective-permute-start(f32[2,8192,128]{2,1,0:T(8,128)} %bitcast.11), channel_id=1, source_target_pairs={{0,64},{64,0},{1,65},{65,1},{2,66},{66,2},{3,67},{67,3},{4,68},{68... | collective-permute-start | bytes 25165832 | tf_op jit(solution)/shard_map/ppermute | solution.py:187
  3.1 30.0 %all-to-all-start = ((f32[128,1,2176]{2,1,0:T(1,128)}), f32[128,1,2176]{2,1,0:T(1,128)S(1)}, u32[]{:S(2)}, u32[]{:S(2)}) async-start(f32[128,1,2176]{2,1,0:T(1,128)} %bitcast.13), calls=%async_computation | async-start | bytes 2228224 | tf_op jit(solution)/shard_map/all_to_all | solution.py:190
  14.3 1.5 %collective-permute-start.1 = (f32[2,8192]{1,0:T(2,128)}, f32[2,8192]{1,0:T(2,128)S(1)}, u32[]{:S(2)}, u32[]{:S(2)}) collective-permute-start(f32[2,8192]{1,0:T(2,128)} %bitcast.16), channel_id=1, source_target_pairs={{0,64},{64,0},{1,65},{65,1},{2,66},{66,2},{3,67},{67,3},{4,68},{68... | collective-permute-start | bytes 196616 | tf_op jit(solution)/shard_map/ppermute | solution.py:188
  15.9 17.2 %copy-start.1 = (f32[2,8192]{1,0:T(2,128)}, f32[2,8192]{1,0:T(2,128)S(1)}, u32[]{:S(2)}) copy-start(f32[2,8192]{1,0:T(2,128)S(1)} %collective-permute-done.1.got_acc_ref) | copy-start | bytes 196612
  33.1 1.1 %copy-start = (f32[128,1,2176]{2,1,0:T(1,128)}, f32[128,1,2176]{2,1,0:T(1,128)S(1)}, u32[]{:S(2)}) copy-start(f32[128,1,2176]{2,1,0:T(1,128)S(1)} %all-to-all-done) | copy-start | bytes 3342340

commit v2 on v1

--- a/solution.py
+++ b/solution.py
@@ -53,13 +53,14 @@
     *scratch,
 ):
     banks = scratch[:BANKS]
-    ids_v, ids_s, in_sem, out_sem, ids_sem = scratch[BANKS:]
+    ids_v, ids_s, spread_ref, in_sem, out_sem, ids_sem = scratch[BANKS:]
     bit = bit_ref[0]
     half_rows = own_ref.shape[1]
     width = own_ref.shape[2]
     senders = rows_ref.shape[0] // (slots + 1)
     stride = slots + 1
     per_half = half_rows // CHUNK
+    blocks = CHUNK // BLOCK
 
     def fetch(src, chunk):
         return pltpu.make_async_copy(
@@ -95,16 +96,26 @@
 
     def gather(sender, carry):
         base = sender * stride
-        for slot in range(slots):
-            row = ids_s[slot, sender]
-            bank = banks[slot % BANKS]
-            bank[pl.ds(row, 1), :] = bank[pl.ds(row, 1), :] + rows_ref[pl.ds(base + slot, 1), :]
+        for slot in range(0, slots, 2):
+            bank = banks[(slot // 2) % BANKS]
+            first = ids_s[slot, sender]
+            second = ids_s[slot + 1, sender]
+            one = rows_ref[pl.ds(base + slot, 1), :]
+            two = rows_ref[pl.ds(base + slot + 1, 1), :]
+            two = jnp.where(first == second, one + two, two)
+            held = bank[pl.ds(first, 1), :]
+            other = bank[pl.ds(second, 1), :]
+            bank[pl.ds(first, 1), :] = held + one
+            bank[pl.ds(second, 1), :] = other + two
         return carry
 
-    lax.fori_loop(0, senders, gather, 0)
-
-    ones = jnp.ones((8, width), jnp.bfloat16)
-    contract = (((1,), (1,)), ((), ()))
+    lax.fori_loop(0, senders, gather, 0, unroll=2)
+
+    lane = lax.broadcasted_iota(jnp.int32, (BLOCK, BLOCK), 1)
+    part = lax.broadcasted_iota(jnp.int32, spread_ref.shape, 0)
+    column = lax.broadcasted_iota(jnp.int32, spread_ref.shape, 1)
+    chosen = (part < 3 * blocks) & (part % blocks == column // BLOCK)
+    spread_ref[...] = jnp.where(chosen, 1.0, 0.0).astype(jnp.bfloat16)
 
     def flush(chunk):
         return pltpu.make_async_copy(
@@ -113,38 +124,55 @@
             out_sem.at[chunk],
         )
 
-    for top in range(2):
-
-        def finish(step, carry, top=top):
-            chunk = top * per_half + step
-            fetch(own_ref, chunk).wait()
-            for block in range(CHUNK // BLOCK):
-                start = pl.multiple_of(chunk * CHUNK + block * BLOCK, BLOCK)
-                at = pl.ds(start, BLOCK)
-                lanes = pl.ds(pl.multiple_of(step * CHUNK + block * BLOCK, BLOCK), BLOCK)
-                total = banks[0][at, :]
-                for bank in banks[1:]:
-                    total = total + bank[at, :]
-                square = total * total
-                high = square.astype(jnp.bfloat16)
-                low = (square - high.astype(jnp.float32)).astype(jnp.bfloat16)
-                summed = lax.dot_general(
-                    ones, high, contract, preferred_element_type=jnp.float32
-                ) + lax.dot_general(ones, low, contract, preferred_element_type=jnp.float32)
-                own = own_acc_ref[:, lanes]
-                got = got_acc_ref[:, lanes]
-                pair = jnp.where(bit == top, own, got)
-                state = jnp.where(bit == 0, pair[0:1, :], pair[1:2, :])
-                state = state + summed[0:1, :] * (1.0 / width)
-                out_acc_ref[pl.ds(top, 1), lanes] = state
-                scale = LEARN_RATE / (jnp.sqrt(state) + EPSILON)
-                scale = jnp.broadcast_to(scale, (BLOCK, BLOCK)).T
-                table[at, :] = table[at, :] - total * scale
-            flush(chunk).start()
-            return carry
-
-        lax.fori_loop(0, per_half, finish, 0)
-
+    def at(chunk, block):
+        return pl.ds(pl.multiple_of(chunk * CHUNK + block * BLOCK, BLOCK), BLOCK)
+
+    def total(where):
+        value = banks[0][where, :]
+        for bank in banks[1:]:
+            value = value + bank[where, :]
+        return value
+
+    def measure(chunk):
+        top = chunk // per_half
+        step = chunk % per_half
+        sums = jnp.zeros((BLOCK, BLOCK), jnp.float32)
+        for block in range(blocks):
+            value = total(at(chunk, block))
+            summed = jnp.sum(value * value, axis=1, keepdims=True)
+            sums = jnp.where(lane == block, summed, sums)
+        picked = pl.ds(2 * blocks * step + bit, blocks, stride=2)
+        state = jnp.where(bit == top, own_acc_ref[picked, :], got_acc_ref[picked, :])
+        state = state + sums.T[:blocks, :] * (1.0 / width)
+        out_acc_ref[pl.ds(2 * blocks * step + top, blocks, stride=2), :] = state
+        return LEARN_RATE / (jnp.sqrt(state) + EPSILON)
+
+    def apply(chunk, scale):
+        high = scale.astype(jnp.bfloat16).astype(jnp.float32)
+        rest = scale - high
+        middle = rest.astype(jnp.bfloat16).astype(jnp.float32)
+        filler = jnp.zeros((BLOCK - 3 * blocks, BLOCK), jnp.float32)
+        parts = jnp.concatenate([high, middle, rest - middle, filler], 0).T
+        wide = jnp.dot(
+            parts.astype(jnp.bfloat16), spread_ref[...], preferred_element_type=jnp.float32
+        )
+        for block in range(blocks):
+            where = at(chunk, block)
+            factor = wide[:, block * BLOCK : (block + 1) * BLOCK]
+            table[where, :] = table[where, :] - total(where) * factor
+
+    def finish(chunk, scale):
+        fetch(own_ref, chunk).wait()
+        following = measure(chunk + 1)
+        apply(chunk, scale)
+        flush(chunk).start()
+        return following
+
+    last = 2 * per_half - 1
+    scale = lax.fori_loop(0, last, finish, measure(0))
+    fetch(own_ref, last).wait()
+    apply(last, scale)
+    flush(last).start()
     for chunk in range(2 * per_half):
         flush(chunk).wait()
 
@@ -160,7 +188,7 @@
         functools.partial(update_kernel, slots),
         out_shape=(
             jax.ShapeDtypeStruct((halves * half_rows, width), jnp.float32),
-            jax.ShapeDtypeStruct((halves, half_rows), jnp.float32),
+            jax.ShapeDtypeStruct(own_acc.shape, jnp.float32),
         ),
         in_specs=[smem, hbm, hbm, vmem, vmem, vmem],
         out_specs=(hbm, vmem),
@@ -169,11 +197,12 @@
             *[pltpu.VMEM((halves * half_rows + 8, width), jnp.float32) for _ in range(BANKS)],
             pltpu.VMEM((slots, senders), jnp.int32),
             pltpu.SMEM((slots, senders), jnp.int32),
+            pltpu.VMEM((BLOCK, CHUNK), jnp.bfloat16),
             pltpu.SemaphoreType.DMA((chunks,)),
             pltpu.SemaphoreType.DMA((chunks,)),
             pltpu.SemaphoreType.DMA,
         ],
-        compiler_params=pltpu.CompilerParams(vmem_limit_bytes=60 * 1024 * 1024),
+        compiler_params=pltpu.CompilerParams(vmem_limit_bytes=48 * 1024 * 1024),
         name="update",
     )(bit, own, got, own_acc, got_acc, rows)
 
@@ -183,7 +212,8 @@
     halves, half_rows = weights.shape[2:4]
     swap = [(0, 1), (1, 0)]
     table = weights[0, 0]
-    state = accum[0, 0]
+    state = accum[0, 0].reshape(halves, half_rows // BLOCK, BLOCK)
+    state = state.transpose(1, 0, 2).reshape(-1, BLOCK)
     got = lax.ppermute(table, "half", swap)
     got_acc = lax.ppermute(state, "half", swap)
     packed = pack(grads[0], row_ids[0], counts, halves * half_rows)
@@ -196,6 +226,7 @@
     ).reshape(owners * (slots + 1), width)
     bit = lax.axis_index("half").astype(jnp.int32).reshape(1)
     new_weights, new_accum = update(bit, table, got, state, got_acc, rows, slots)
+    new_accum = new_accum.reshape(half_rows // BLOCK, halves, BLOCK).transpose(1, 0, 2)
     return (
         new_weights.reshape(1, 1, halves, half_rows, width),
         new_accum.reshape(1, 1, halves, half_rows),

time: 53.3 us -> 46.6 us (0.87)
  Pallas kernels: 21.2 us -> 14.9 us
    pallas_call x1, Pallas kernels: 18.9 us -> 12.6 us  [update(): pl.pallas_call(functools.partial(update_kernel, slots), out_shape=(jax.Sh...]
    unnamed x4 -> x2, local copies, waits for them, and re-layouts: 1.08 us -> 0.84 us
  transfers between devices with their start and end apart: 3 -> 3, of which waited for: 2 -> 2; matrix products, arithmetic and copies ran while one was open for 0% -> 0% of each run, Pallas kernels for 4% -> 5%
where the time goes in v2:
time: 46.6 us; the launch traced here: 46.5 us
  waiting for transfers between devices  18.7 us (40%)
  Pallas kernels  14.9 us (32%)
  starting transfers between devices  11.4 us (24%)
  local copies, waits for them, and re-layouts  0.84 us (2%)
  between operations  0.66 us (1%)
    all_to_all x1, waiting for transfers between devices, per_device(): lax.all_to_all(packed.reshape(owners, 1, (slots + 1) * width), ('half', '...  17.2 us
    pallas_call x1, Pallas kernels, update(): pl.pallas_call(functools.partial(update_kernel, slots), out_shape=(jax.Sh...  12.6 us
    all_to_all x1, starting transfers between devices, per_device(): lax.all_to_all(packed.reshape(owners, 1, (slots + 1) * width), ('half', '...  11.3 us
    pallas_call x1, Pallas kernels, pack(): pl.pallas_call(functools.partial(pack_kernel, slots, dead), out_shape=jax...  2.34 us
    ppermute x1, waiting for transfers between devices, per_device(): got_acc = lax.ppermute(state, 'half', swap)  1.45 us
  transfers between devices with their start and end apart: 3, of which 2 were waited for; matrix products, arithmetic and copies ran while one was open for 0% of the time, Pallas kernels for 5%

profile of v2, /device:TPU:0, one launch (start us, length us, event | category | flops | bytes accessed | tf_op | source)
XLA Modules:
  0.0 46.5 jit_solution(17497917335002618430)
XLA Ops:
  0.6 0.1 collective-permute-start
  0.7 2.3 %pack.1 = f32[2176,128]{1,0:T(8,128)} custom-call(f32[2048,128]{1,0:T(8,128)} %bitcast.25, s32[16,128]{1,0:T(8,128)} %bitcast.26, s32[1,128]{1,0:T(1,128)} %counts_ref.1), custom_call_target="tpu_custom_call" | custom-call | tf_op jit(solution)/shard_map/pack/pallas_call | solution.py:33
  3.1 11.3 %all-to-all-start = ((f32[128,1,2176]{2,1,0:T(1,128)}), f32[128,1,2176]{2,1,0:T(1,128)S(1)}, u32[]{:S(2)}, u32[]{:S(2)}) async-start(f32[128,1,2176]{2,1,0:T(1,128)} %bitcast.24), calls=%async_computation | async-start | bytes 2228224 | tf_op jit(solution)/shard_map/all_to_all | solution.py:220
  14.3 0.1 collective-permute-start.1
  14.4 1.4 %collective-permute-done.1.got_acc_ref = f32[128,128]{1,0:T(8,128)S(1)} collective-permute-done((f32[128,128]{1,0:T(8,128)}, f32[128,128]{1,0:T(8,128)S(1)}, u32[]{:S(2)}, u32[]{:S(2)}) %collective-permute-start.1) | collective-permute-done | bytes 65568 | tf_op jit(solution)/shard_map/ppermute | solution.py:218
  15.9 17.2 %all-to-all-done = f32[128,1,2176]{2,1,0:T(1,128)S(1)} async-done(((f32[128,1,2176]{2,1,0:T(1,128)}), f32[128,1,2176]{2,1,0:T(1,128)S(1)}, u32[]{:S(2)}, u32[]{:S(2)}) %all-to-all-start) | async-done | bytes 1114144 | tf_op jit(solution)/shard_map/all_to_all | solution.py:220
  33.1 0.0 collective-permute-done.got_ref
  33.1 0.0 copy-start
  33.1 0.8 %copy-done = f32[1,1,2,8192]{3,2,1,0:T(2,128)S(1)} copy-done((f32[1,1,2,8192]{3,2,1,0:T(2,128)S(1)}, f32[1,1,2,8192]{3,2,1,0:T(2,128)}, u32[]{:S(2)}) %copy-start) | copy-done | bytes 65560
  33.9 12.6 %update.1 = (f32[16384,128]{1,0:T(8,128)}, f32[128,128]{1,0:T(8,128)}) custom-call(s32[1]{0:T(128)} %bitcast.bit_ref, f32[2,8192,128]{2,1,0:T(8,128)} %bitcast.23, f32[2,8192,128]{2,1,0:T(8,128)} %collective-permute-done.got_ref, f32[128,128]{1,0:T(8,128)S(1)} %bitcast.21, f32[128,128]{1,0:T(8,128)S(1)} %collective-permute-done.1.got_acc_ref, ...), custom_call_target="tpu_custom_call" | custom-call | tf_op jit(solution)/shard_map/update/pallas_call | solution.py:187
Async XLA Ops:
  0.6 32.5 %collective-permute-start = (f32[2,8192,128]{2,1,0:T(8,128)}, f32[2,8192,128]{2,1,0:T(8,128)}, u32[]{:S(2)}, u32[]{:S(2)}) collective-permute-start(f32[2,8192,128]{2,1,0:T(8,128)} %bitcast.22), channel_id=1, source_target_pairs={{0,64},{64,0},{1,65},{65,1},{2,66},{66,2},{3,67},{67,3},{4,68},{68... | collective-permute-start | bytes 25165832 | tf_op jit(solution)/shard_map/ppermute | solution.py:217
  3.1 30.0 %all-to-all-start = ((f32[128,1,2176]{2,1,0:T(1,128)}), f32[128,1,2176]{2,1,0:T(1,128)S(1)}, u32[]{:S(2)}, u32[]{:S(2)}) async-start(f32[128,1,2176]{2,1,0:T(1,128)} %bitcast.24), calls=%async_computation | async-start | bytes 2228224 | tf_op jit(solution)/shard_map/all_to_all | solution.py:220
  14.3 1.5 %collective-permute-start.1 = (f32[128,128]{1,0:T(8,128)}, f32[128,128]{1,0:T(8,128)S(1)}, u32[]{:S(2)}, u32[]{:S(2)}) collective-permute-start(f32[128,128]{1,0:T(8,128)} %bitcast.20), channel_id=1, source_target_pairs={{0,64},{64,0},{1,65},{65,1},{2,66},{66,2},{3,67},{67,3},{4,68},{68... | collective-permute-start | bytes 196616 | tf_op jit(solution)/shard_map/ppermute | solution.py:218
  33.1 0.8 %copy-start = (f32[1,1,2,8192]{3,2,1,0:T(2,128)S(1)}, f32[1,1,2,8192]{3,2,1,0:T(2,128)}, u32[]{:S(2)}) copy-start(f32[1,1,2,8192]{3,2,1,0:T(2,128)} %param.6) | copy-start | bytes 196612

commit v3 on v2

v3 whole, which is shorter than its diff:
```python
import functools

import jax
import jax.numpy as jnp
from jax import lax
from jax.experimental import pallas as pl
from jax.experimental.pallas import tpu as pltpu
from jax.sharding import PartitionSpec as P

LEARN_RATE = 0.5
EPSILON = 1e-06
BLOCK = 128
CHUNK = 1024
PACK_STEPS = 2


def split(value):
    high = value.astype(jnp.bfloat16)
    rest = value - high.astype(jnp.float32)
    middle = rest.astype(jnp.bfloat16)
    low = (rest - middle.astype(jnp.float32)).astype(jnp.bfloat16)
    return high, middle, low


def pack_kernel(slots, dead, grads_ref, ids_ref, counts_ref, out_ref, turned, flat):
    owners = ids_ref.shape[1]
    stride = slots + 1
    group = BLOCK // slots
    step = pl.program_id(0)
    batches = grads_ref.shape[0] // BLOCK

    @pl.when(step == 0)
    def _():
        slot = lax.broadcasted_iota(jnp.int32, ids_ref.shape, 0)
        marked = jnp.where(slot < counts_ref[...], ids_ref[...], dead).astype(jnp.float32)
        filler = jnp.zeros((BLOCK - slots, owners), jnp.float32)
        turned[...] = jnp.concatenate([marked, filler], 0).T
        rows = turned[pl.ds(0, owners // group, stride=group), :]
        for part in range(1, group):
            piece = turned[pl.ds(part, owners // group, stride=group), :]
            rows = rows + pltpu.roll(piece, part * slots, 1)
        flat[...] = rows

    below = lax.broadcasted_iota(jnp.int32, (BLOCK, BLOCK), 0)
    across = lax.broadcasted_iota(jnp.int32, (BLOCK, BLOCK), 1)
    together = below // slots == across // slots
    earlier = together & (below < across)
    for batch in range(batches):
        row = flat[pl.ds(step * batches + batch, 1), :]
        wide = jnp.broadcast_to(row, (BLOCK, BLOCK))
        same = wide == wide.T
        merge = jnp.where(same & together, 1.0, 0.0).astype(jnp.bfloat16)
        seen = jnp.max(jnp.where(same & earlier, 1.0, 0.0), axis=0, keepdims=True)
        kept = jnp.where(seen > 0, float(dead), row)
        merged = jnp.zeros((BLOCK, BLOCK), jnp.float32)
        for part in split(grads_ref[batch * BLOCK : (batch + 1) * BLOCK, :]):
            merged = merged + jnp.dot(merge, part, preferred_element_type=jnp.float32)
        for owner in range(group):
            base = stride * (batch * group + owner)
            out_ref[base : base + slots, :] = merged[owner * slots : (owner + 1) * slots, :]
            out_ref[base + slots : base + stride, :] = kept


def pack(grads, ids, counts, dead):
    owners, slots, width = grads.shape
    steps = PACK_STEPS
    return pl.pallas_call(
        functools.partial(pack_kernel, slots, dead),
        grid=(steps,),
        out_shape=jax.ShapeDtypeStruct((owners * (slots + 1), width), jnp.float32),
        in_specs=[
            pl.BlockSpec((owners * slots // steps, width), lambda step: (step, 0)),
            pl.BlockSpec((slots, owners), lambda step: (0, 0)),
            pl.BlockSpec((1, owners), lambda step: (0, 0)),
        ],
        out_specs=pl.BlockSpec((owners * (slots + 1) // steps, width), lambda step: (step, 0)),
        scratch_shapes=[
            pltpu.VMEM((owners, BLOCK), jnp.float32),
            pltpu.VMEM((owners * slots // BLOCK, BLOCK), jnp.float32),
        ],
        name="pack",
    )(grads.reshape(owners * slots, width), ids.T, counts)


def update_kernel(
    slots,
    bit_ref,
    own_ref,
    got_ref,
    acc_ref,
    rows_ref,
    out_ref,
    out_acc_ref,
    table,
    bank,
    ids_v,
    ids_s,
    spread_ref,
    in_sem,
    out_sem,
    ids_sem,
):
    bit = bit_ref[0]
    place = bit_ref[1]
    half_rows = own_ref.shape[1]
    width = own_ref.shape[2]
    senders = rows_ref.shape[0] // (slots + 1)
    stride = slots + 1
    per_half = half_rows // CHUNK
    blocks = CHUNK // BLOCK

    def fetch(src, chunk):
        return pltpu.make_async_copy(
            src.at[bit, pl.ds((chunk % per_half) * CHUNK, CHUNK), :],
            table.at[pl.ds(chunk * CHUNK, CHUNK), :],
            in_sem.at[chunk],
        )

    group = BLOCK // slots
    sector = lax.broadcasted_iota(jnp.int32, (senders // group, width), 1) // slots
    found = jnp.zeros((senders // group, width), jnp.float32)
    for part in range(group):
        ids = rows_ref[pl.ds(slots + part * stride, senders // group, stride=group * stride), :]
        ids = pltpu.roll(ids, lax.rem(part + group - place, group) * slots, 1)
        found = jnp.where(sector == part, ids, found)
    ids_v[...] = found.astype(jnp.int32)
    to_scalar = pltpu.make_async_copy(ids_v, ids_s, ids_sem)
    to_scalar.start()
    for top in range(2):
        for chunk in range(top * per_half, (top + 1) * per_half):

            @pl.when(bit == top)
            def _():
                fetch(own_ref, chunk).start()

            @pl.when(bit != top)
            def _():
                fetch(got_ref, chunk).start()

    zero = jnp.zeros((256, width), jnp.float32)

    def clear(step, carry):
        bank[pl.ds(pl.multiple_of(step * 256, 256), 256), :] = zero
        return carry

    lax.fori_loop(0, 2 * half_rows // 256, clear, 0)
    part = lax.broadcasted_iota(jnp.int32, spread_ref.shape, 0)
    column = lax.broadcasted_iota(jnp.int32, spread_ref.shape, 1)
    chosen = (part < 3 * blocks) & (part % blocks == column // BLOCK)
    spread_ref[...] = jnp.where(chosen, 1.0, 0.0).astype(jnp.bfloat16)
    to_scalar.wait()

    def gather(step, carry):
        for part in range(group):
            base = (step * group + part) * stride
            targets = [ids_s[step, part * slots + slot] for slot in range(slots)]
            held = [bank[pl.ds(target, 1), :] for target in targets]
            held = [old + rows_ref[pl.ds(base + slot, 1), :] for slot, old in enumerate(held)]
            for target, new in zip(targets, held):
                bank[pl.ds(target, 1), :] = new
        return carry

    lax.fori_loop(0, senders // group, gather, 0)

    lane = lax.broadcasted_iota(jnp.int32, (BLOCK, BLOCK), 1)
    def flush(chunk):
        return pltpu.make_async_copy(
            table.at[pl.ds(chunk * CHUNK, CHUNK), :],
            out_ref.at[pl.ds(chunk * CHUNK, CHUNK), :],
            out_sem.at[chunk],
        )

    def at(chunk, block):
        return pl.ds(pl.multiple_of(chunk * CHUNK + block * BLOCK, BLOCK), BLOCK)

    def measure(chunk):
        top = chunk // per_half
        step = chunk % per_half
        sums = jnp.zeros((BLOCK, BLOCK), jnp.float32)
        for block in range(blocks):
            value = bank[at(chunk, block), :]
            summed = jnp.sum(value * value, axis=1, keepdims=True)
            sums = jnp.where(lane == block, summed, sums)
        picked = pl.ds(2 * blocks * step + top, blocks, stride=2)
        state = acc_ref[picked, :]
        state = state + sums.T[:blocks, :] * (1.0 / width)
        out_acc_ref[picked, :] = state
        return LEARN_RATE / (jnp.sqrt(state) + EPSILON)

    def apply(chunk, scale):
        filler = jnp.zeros((BLOCK - 3 * blocks, BLOCK), jnp.float32)
        parts = [part.astype(jnp.float32) for part in split(scale)]
        parts = jnp.concatenate([*parts, filler], 0).T
        wide = jnp.dot(
            parts.astype(jnp.bfloat16), spread_ref[...], preferred_element_type=jnp.float32
        )
        for block in range(blocks):
            where = at(chunk, block)
            factor = wide[:, block * BLOCK : (block + 1) * BLOCK]
            table[where, :] = table[where, :] - bank[where, :] * factor

    def finish(chunk, scale):
        fetch(own_ref, chunk).wait()
        following = measure(chunk + 1)
        apply(chunk, scale)
        flush(chunk).start()
        return following

    last = 2 * per_half - 1
    scale = lax.fori_loop(0, last, finish, measure(0))
    fetch(own_ref, last).wait()
    apply(last, scale)
    flush(last).start()
    for chunk in range(2 * per_half):
        flush(chunk).wait()


def update(place, own, got, acc, rows, slots):
    halves, half_rows, width = own.shape
    senders = rows.shape[0] // (slots + 1)
    chunks = halves * half_rows // CHUNK
    vmem = pl.BlockSpec(memory_space=pltpu.VMEM)
    hbm = pl.BlockSpec(memory_space=pltpu.HBM)
    smem = pl.BlockSpec(memory_space=pltpu.SMEM)
    return pl.pallas_call(
        functools.partial(update_kernel, slots),
        out_shape=(
            jax.ShapeDtypeStruct((halves * half_rows, width), jnp.float32),
            jax.ShapeDtypeStruct(acc.shape, jnp.float32),
        ),
        in_specs=[smem, hbm, hbm, vmem, vmem],
        out_specs=(hbm, vmem),
        scratch_shapes=[
            pltpu.VMEM((halves * half_rows, width), jnp.float32),
            pltpu.VMEM((halves * half_rows + 8, width), jnp.float32),
            pltpu.VMEM((senders * slots // width, width), jnp.int32),
            pltpu.SMEM((senders * slots // width, width), jnp.int32),
            pltpu.VMEM((BLOCK, CHUNK), jnp.bfloat16),
            pltpu.SemaphoreType.DMA((chunks,)),
            pltpu.SemaphoreType.DMA((chunks,)),
            pltpu.SemaphoreType.DMA,
        ],
        compiler_params=pltpu.CompilerParams(vmem_limit_bytes=48 * 1024 * 1024),
        name="update",
    )(place, own, got, acc, rows)


def per_device(weights, accum, grads, row_ids, counts):
    owners, slots, width = grads.shape[1:]
    halves, half_rows = weights.shape[2:4]
    swap = [(0, 1), (1, 0)]
    table = weights[0, 0]
    bit = lax.axis_index("half").astype(jnp.int32)
    state = accum[0, 0].reshape(halves, half_rows // BLOCK, BLOCK).transpose(1, 0, 2)
    got = lax.ppermute(table, "half", swap)
    got_acc = lax.ppermute(state, "half", swap)
    packed = pack(grads[0], row_ids[0], counts, halves * half_rows)
    rows = lax.all_to_all(
        packed.reshape(owners, 1, (slots + 1) * width),
        ("half", "grp"),
        split_axis=0,
        concat_axis=0,
        tiled=True,
    ).reshape(owners * (slots + 1), width)
    mine = jnp.where(bit == 0, state[:, 0], state[:, 1])
    theirs = jnp.where(bit == 0, got_acc[:, 0], got_acc[:, 1])
    acc = jnp.stack([jnp.where(bit == 0, mine, theirs), jnp.where(bit == 0, theirs, mine)], 1)
    group = BLOCK // slots
    place = jnp.stack([bit, lax.rem(lax.axis_index("grp").astype(jnp.int32), group)])
    new_weights, new_accum = update(place, table, got, acc.reshape(-1, BLOCK), rows, slots)
    new_accum = new_accum.reshape(half_rows // BLOCK, halves, BLOCK).transpose(1, 0, 2)
    return (
        new_weights.reshape(1, 1, halves, half_rows, width),
        new_accum.reshape(1, 1, halves, half_rows),
    )


def solution(mesh):
    placed = (
        P("half", "grp", None, None, None),
        P("half", "grp", None, None),
        P(("half", "grp"), None, None, None),
        P(("half", "grp"), None, None),
        P(("half", "grp"), None),
    )
    return jax.shard_map(
        per_device,
        mesh=mesh,
        in_specs=placed,
        out_specs=(P("half", "grp", None, None, None), P("half", "grp", None, None)),
        check_vma=False,
    )
```

time: 46.6 us -> 45.1 us (0.968)
  waiting for transfers between devices: 18.7 us -> 17.5 us
  other arithmetic: 0 us -> 1.14 us
  local copies, waits for them, and re-layouts: 0.84 us -> 0 us
  Pallas kernels: 14.9 us -> 14.1 us
    pallas_call x1, Pallas kernels: 12.6 us -> 11.1 us  [update(): pl.pallas_call(functools.partial(update_kernel, slots), out_shape=(jax.Sh...]
    all_to_all x1, waiting for transfers between devices: 17.2 us -> 16.1 us  [per_device(): lax.all_to_all(packed.reshape(owners, 1, (slots + 1) * width), ('half', '...]
    select_n x0 -> x1, other arithmetic: none -> 1 us  [per_device(): jnp.where(bit == 0, mine, theirs)]
    unnamed x2 -> x0, local copies, waits for them, and re-layouts: 0.84 us -> none
    pallas_call x1, Pallas kernels: 2.34 us -> 2.98 us  [pack(): pl.pallas_call(functools.partial(pack_kernel, slots, dead), grid=(steps,)...]
  transfers between devices with their start and end apart: 3 -> 3, of which waited for: 2 -> 2; matrix products, arithmetic and copies ran while one was open for 0% -> 3% of each run, Pallas kernels for 5% -> 7%
where the time goes in v3:
time: 45.1 us; the launch traced here: 44.9 us
  waiting for transfers between devices  17.5 us (39%)
  Pallas kernels  14.1 us (31%)
  starting transfers between devices  11.4 us (25%)
  other arithmetic  1.14 us (3%)
  between operations  0.67 us (1%)
    all_to_all x1, waiting for transfers between devices, per_device(): lax.all_to_all(packed.reshape(owners, 1, (slots + 1) * width), ('half', '...  16.1 us
    all_to_all x1, starting transfers between devices, per_device(): lax.all_to_all(packed.reshape(owners, 1, (slots + 1) * width), ('half', '...  11.3 us
    pallas_call x1, Pallas kernels, update(): pl.pallas_call(functools.partial(update_kernel, slots), out_shape=(jax.Sh...  11.1 us
    pallas_call x1, Pallas kernels, pack(): pl.pallas_call(functools.partial(pack_kernel, slots, dead), grid=(steps,)...  2.98 us
    ppermute x1, waiting for transfers between devices, per_device(): got_acc = lax.ppermute(state, 'half', swap)  1.37 us
    select_n x1, other arithmetic, per_device(): jnp.where(bit == 0, mine, theirs)  1 us
  transfers between devices with their start and end apart: 3, of which 2 were waited for; matrix products, arithmetic and copies ran while one was open for 3% of the time, Pallas kernels for 7%

profile of v3, /device:TPU:0, one launch (start us, length us, event | category | flops | bytes accessed | tf_op | source)
XLA Modules:
  0.0 44.9 jit_solution(2186467214096998657)
XLA Ops:
  0.6 0.1 collective-permute-start
  0.7 3.0 %pack.1 = f32[2176,128]{1,0:T(8,128)} custom-call(f32[2048,128]{1,0:T(8,128)} %bitcast.24, s32[16,128]{1,0:T(8,128)} %bitcast.27, s32[1,128]{1,0:T(1,128)} %counts_ref.1), custom_call_target="tpu_custom_call" | custom-call | tf_op jit(solution)/shard_map/pack/pallas_call | solution.py:67
  3.7 11.3 %all-to-all-start = ((f32[128,1,2176]{2,1,0:T(1,128)}), f32[128,1,2176]{2,1,0:T(1,128)S(1)}, u32[]{:S(2)}, u32[]{:S(2)}) async-start(f32[128,1,2176]{2,1,0:T(1,128)} %bitcast.23), calls=%async_computation | async-start | bytes 2228224 | tf_op jit(solution)/shard_map/all_to_all | solution.py:258
  15.0 0.1 collective-permute-start.1
  15.1 0.1 pad_add_fusion.bit_ref
  15.2 1.4 %collective-permute-done.1 = f32[64,2,128]{2,1,0:T(2,128)S(1)} collective-permute-done((f32[64,2,128]{2,1,0:T(2,128)}, f32[64,2,128]{2,1,0:T(2,128)S(1)}, u32[]{:S(2)}, u32[]{:S(2)}) %collective-permute-start.1) | collective-permute-done | bytes 65568 | tf_op jit(solution)/shard_map/ppermute | solution.py:256
  16.5 1.0 %broadcast_select_fusion.1 = (f32[64,1,128]{2,1,0:T(1,128)S(1)}, f32[64,1,128]{2,1,0:T(1,128)S(1)}) fusion(pred[]{:T(512)S(6)} %eq.2, f32[64,2,128]{2,1,0:T(2,128)} %bitcast.26, f32[64,2,128]{2,1,0:T(2,128)S(1)} %collective-permute-done.1), kind=kLoop, calls=%fused_computation.2 | loop fusion | flops 32768 | bytes 196609 | tf_op jit(solution)/shard_map/jit(_where)/select_n | solution.py:267
  17.5 0.1 pad_maximum_fusion
  17.6 16.1 %all-to-all-done = f32[128,1,2176]{2,1,0:T(1,128)S(1)} async-done(((f32[128,1,2176]{2,1,0:T(1,128)}), f32[128,1,2176]{2,1,0:T(1,128)S(1)}, u32[]{:S(2)}, u32[]{:S(2)}) %all-to-all-start) | async-done | bytes 1114144 | tf_op jit(solution)/shard_map/all_to_all | solution.py:258
  33.7 0.0 collective-permute-done.got_ref
  33.7 11.1 %update.1 = (f32[16384,128]{1,0:T(8,128)}, f32[128,128]{1,0:T(8,128)}) custom-call(s32[2]{0:T(128)S(1)} %pad_add_fusion.bit_ref, f32[2,8192,128]{2,1,0:T(8,128)} %bitcast.22, f32[2,8192,128]{2,1,0:T(8,128)} %collective-permute-done.got_ref, f32[128,128]{1,0:T(8,128)S(1)} %bitcast.20, f32[2176,128]{1,0:T(8,128)S(1)} %bitcast.19), custom_call_target="tpu_custom_call" | custom-call | tf_op jit(solution)/shard_map/update/pallas_call | solution.py:225
Async XLA Ops:
  0.6 33.1 %collective-permute-start = (f32[2,8192,128]{2,1,0:T(8,128)}, f32[2,8192,128]{2,1,0:T(8,128)}, u32[]{:S(2)}, u32[]{:S(2)}) collective-permute-start(f32[2,8192,128]{2,1,0:T(8,128)} %bitcast.21), channel_id=1, source_target_pairs={{0,64},{64,0},{1,65},{65,1},{2,66},{66,2},{3,67},{67,3},{4,68},{68... | collective-permute-start | bytes 25165832 | tf_op jit(solution)/shard_map/ppermute | solution.py:255
  3.7 30.0 %all-to-all-start = ((f32[128,1,2176]{2,1,0:T(1,128)}), f32[128,1,2176]{2,1,0:T(1,128)S(1)}, u32[]{:S(2)}, u32[]{:S(2)}) async-start(f32[128,1,2176]{2,1,0:T(1,128)} %bitcast.23), calls=%async_computation | async-start | bytes 2228224 | tf_op jit(solution)/shard_map/all_to_all | solution.py:258
  15.0 1.5 %collective-permute-start.1 = (f32[64,2,128]{2,1,0:T(2,128)}, f32[64,2,128]{2,1,0:T(2,128)S(1)}, u32[]{:S(2)}, u32[]{:S(2)}) collective-permute-start(f32[64,2,128]{2,1,0:T(2,128)} %bitcast.25), channel_id=1, source_target_pairs={{0,64},{64,0},{1,65},{65,1},{2,66},{66,2},{3,67},{67,3},{4,68},{68... | collective-permute-start | bytes 196616 | tf_op jit(solution)/shard_map/ppermute | solution.py:256

commit v4 on v3

--- a/solution.py
+++ b/solution.py
@@ -84,7 +84,6 @@
 
 def update_kernel(
     slots,
-    bit_ref,
     own_ref,
     got_ref,
     acc_ref,
@@ -93,15 +92,17 @@
     out_acc_ref,
     table,
     bank,
+    states,
     ids_v,
     ids_s,
     spread_ref,
     in_sem,
     out_sem,
     ids_sem,
+    acc_sem,
 ):
-    bit = bit_ref[0]
-    place = bit_ref[1]
+    bit = lax.axis_index("half").astype(jnp.int32)
+    place = lax.rem(lax.axis_index("grp").astype(jnp.int32), BLOCK // slots)
     half_rows = own_ref.shape[1]
     width = own_ref.shape[2]
     senders = rows_ref.shape[0] // (slots + 1)
@@ -184,7 +185,7 @@
         picked = pl.ds(2 * blocks * step + top, blocks, stride=2)
         state = acc_ref[picked, :]
         state = state + sums.T[:blocks, :] * (1.0 / width)
-        out_acc_ref[picked, :] = state
+        states[picked, :] = state
         return LEARN_RATE / (jnp.sqrt(state) + EPSILON)
 
     def apply(chunk, scale):
@@ -208,41 +209,45 @@
 
     last = 2 * per_half - 1
     scale = lax.fori_loop(0, last, finish, measure(0))
+    states_out = pltpu.make_async_copy(states, out_acc_ref, acc_sem)
+    states_out.start()
     fetch(own_ref, last).wait()
     apply(last, scale)
     flush(last).start()
     for chunk in range(2 * per_half):
         flush(chunk).wait()
-
-
-def update(place, own, got, acc, rows, slots):
+    states_out.wait()
+
+
+def update(own, got, acc, rows, slots):
     halves, half_rows, width = own.shape
     senders = rows.shape[0] // (slots + 1)
     chunks = halves * half_rows // CHUNK
     vmem = pl.BlockSpec(memory_space=pltpu.VMEM)
     hbm = pl.BlockSpec(memory_space=pltpu.HBM)
-    smem = pl.BlockSpec(memory_space=pltpu.SMEM)
     return pl.pallas_call(
         functools.partial(update_kernel, slots),
         out_shape=(
             jax.ShapeDtypeStruct((halves * half_rows, width), jnp.float32),
             jax.ShapeDtypeStruct(acc.shape, jnp.float32),
         ),
-        in_specs=[smem, hbm, hbm, vmem, vmem],
-        out_specs=(hbm, vmem),
+        in_specs=[hbm, hbm, vmem, vmem],
+        out_specs=(hbm, hbm),
         scratch_shapes=[
             pltpu.VMEM((halves * half_rows, width), jnp.float32),
             pltpu.VMEM((halves * half_rows + 8, width), jnp.float32),
+            pltpu.VMEM(acc.shape, jnp.float32),
             pltpu.VMEM((senders * slots // width, width), jnp.int32),
             pltpu.SMEM((senders * slots // width, width), jnp.int32),
             pltpu.VMEM((BLOCK, CHUNK), jnp.bfloat16),
             pltpu.SemaphoreType.DMA((chunks,)),
             pltpu.SemaphoreType.DMA((chunks,)),
             pltpu.SemaphoreType.DMA,
+            pltpu.SemaphoreType.DMA,
         ],
         compiler_params=pltpu.CompilerParams(vmem_limit_bytes=48 * 1024 * 1024),
         name="update",
-    )(place, own, got, acc, rows)
+    )(own, got, acc, rows)
 
 
 def per_device(weights, accum, grads, row_ids, counts):
@@ -265,9 +270,7 @@
     mine = jnp.where(bit == 0, state[:, 0], state[:, 1])
     theirs = jnp.where(bit == 0, got_acc[:, 0], got_acc[:, 1])
     acc = jnp.stack([jnp.where(bit == 0, mine, theirs), jnp.where(bit == 0, theirs, mine)], 1)
-    group = BLOCK // slots
-    place = jnp.stack([bit, lax.rem(lax.axis_index("grp").astype(jnp.int32), group)])
-    new_weights, new_accum = update(place, table, got, acc.reshape(-1, BLOCK), rows, slots)
+    new_weights, new_accum = update(table, got, acc.reshape(-1, BLOCK), rows, slots)
     new_accum = new_accum.reshape(half_rows // BLOCK, halves, BLOCK).transpose(1, 0, 2)
     return (
         new_weights.reshape(1, 1, halves, half_rows, width),

time: 45.1 us -> 43.9 us (0.973)
  Pallas kernels: 14.1 us -> 13 us
    pallas_call x1, Pallas kernels: 11.1 us -> 9.97 us  [update(): pl.pallas_call(functools.partial(update_kernel, slots), out_shape=(jax.Sh...]
  transfers between devices with their start and end apart: 3 -> 3, of which waited for: 2 -> 2; matrix products, arithmetic and copies ran while one was open for 3% -> 2% of each run, Pallas kernels for 7% -> 7%
where the time goes in v4:
time: 43.9 us; the launch traced here: 43.7 us
  waiting for transfers between devices  17.6 us (40%)
  Pallas kernels  13 us (30%)
  starting transfers between devices  11.4 us (26%)
  other arithmetic  1.06 us (2%)
  between operations  0.67 us (2%)
    all_to_all x1, waiting for transfers between devices, per_device(): lax.all_to_all(packed.reshape(owners, 1, (slots + 1) * width), ('half', '...  16.1 us
    all_to_all x1, starting transfers between devices, per_device(): lax.all_to_all(packed.reshape(owners, 1, (slots + 1) * width), ('half', '...  11.3 us
    pallas_call x1, Pallas kernels, update(): pl.pallas_call(functools.partial(update_kernel, slots), out_shape=(jax.Sh...  9.97 us
    pallas_call x1, Pallas kernels, pack(): pl.pallas_call(functools.partial(pack_kernel, slots, dead), grid=(steps,)...  2.98 us
    ppermute x1, waiting for transfers between devices, per_device(): got_acc = lax.ppermute(state, 'half', swap)  1.44 us
    select_n x1, other arithmetic, per_device(): jnp.where(bit == 0, mine, theirs)  1 us
  transfers between devices with their start and end apart: 3, of which 2 were waited for; matrix products, arithmetic and copies ran while one was open for 2% of the time, Pallas kernels for 7%

profile of v4, /device:TPU:0, one launch (start us, length us, event | category | flops | bytes accessed | tf_op | source)
XLA Modules:
  0.0 43.7 jit_solution(3362278859829805302)
XLA Ops:
  0.6 0.1 collective-permute-start
  0.7 3.0 %pack.1 = f32[2176,128]{1,0:T(8,128)} custom-call(f32[2048,128]{1,0:T(8,128)} %bitcast.22, s32[16,128]{1,0:T(8,128)} %bitcast.25, s32[1,128]{1,0:T(1,128)} %counts_ref.1), custom_call_target="tpu_custom_call" | custom-call | tf_op jit(solution)/shard_map/pack/pallas_call | solution.py:67
  3.7 11.3 %all-to-all-start = ((f32[128,1,2176]{2,1,0:T(1,128)}), f32[128,1,2176]{2,1,0:T(1,128)S(1)}, u32[]{:S(2)}, u32[]{:S(2)}) async-start(f32[128,1,2176]{2,1,0:T(1,128)} %bitcast.21), calls=%async_computation | async-start | bytes 2228224 | tf_op jit(solution)/shard_map/all_to_all | solution.py:263
  15.0 0.1 collective-permute-start.1
  15.1 1.4 %collective-permute-done.1 = f32[64,2,128]{2,1,0:T(2,128)S(1)} collective-permute-done((f32[64,2,128]{2,1,0:T(2,128)}, f32[64,2,128]{2,1,0:T(2,128)S(1)}, u32[]{:S(2)}, u32[]{:S(2)}) %collective-permute-start.1) | collective-permute-done | bytes 65568 | tf_op jit(solution)/shard_map/ppermute | solution.py:261
  16.5 1.0 %broadcast_select_fusion.1 = (f32[64,1,128]{2,1,0:T(1,128)S(1)}, f32[64,1,128]{2,1,0:T(1,128)S(1)}) fusion(pred[]{:T(512)S(6)} %eq.2, f32[64,2,128]{2,1,0:T(2,128)} %bitcast.24, f32[64,2,128]{2,1,0:T(2,128)S(1)} %collective-permute-done.1), kind=kLoop, calls=%fused_computation.2 | loop fusion | flops 32768 | bytes 196609 | tf_op jit(solution)/shard_map/jit(_where)/select_n | solution.py:272
  17.5 0.1 pad_maximum_fusion
  17.6 16.1 %all-to-all-done = f32[128,1,2176]{2,1,0:T(1,128)S(1)} async-done(((f32[128,1,2176]{2,1,0:T(1,128)}), f32[128,1,2176]{2,1,0:T(1,128)S(1)}, u32[]{:S(2)}, u32[]{:S(2)}) %all-to-all-start) | async-done | bytes 1114144 | tf_op jit(solution)/shard_map/all_to_all | solution.py:263
  33.7 0.0 collective-permute-done.got_ref
  33.7 10.0 %update.1 = (f32[16384,128]{1,0:T(8,128)}, f32[128,128]{1,0:T(8,128)}) custom-call(f32[2,8192,128]{2,1,0:T(8,128)} %bitcast.20, f32[2,8192,128]{2,1,0:T(8,128)} %collective-permute-done.got_ref, f32[128,128]{1,0:T(8,128)S(1)} %bitcast.18, f32[2176,128]{1,0:T(8,128)S(1)} %bitcast.17), custom_call_target="tpu_custom_call" | custom-call | tf_op jit(solution)/shard_map/update/pallas_call | solution.py:228
Async XLA Ops:
  0.6 33.1 %collective-permute-start = (f32[2,8192,128]{2,1,0:T(8,128)}, f32[2,8192,128]{2,1,0:T(8,128)}, u32[]{:S(2)}, u32[]{:S(2)}) collective-permute-start(f32[2,8192,128]{2,1,0:T(8,128)} %bitcast.19), channel_id=1, source_target_pairs={{0,64},{64,0},{1,65},{65,1},{2,66},{66,2},{3,67},{67,3},{4,68},{68... | collective-permute-start | bytes 25165832 | tf_op jit(solution)/shard_map/ppermute | solution.py:260
  3.7 30.0 %all-to-all-start = ((f32[128,1,2176]{2,1,0:T(1,128)}), f32[128,1,2176]{2,1,0:T(1,128)S(1)}, u32[]{:S(2)}, u32[]{:S(2)}) async-start(f32[128,1,2176]{2,1,0:T(1,128)} %bitcast.21), calls=%async_computation | async-start | bytes 2228224 | tf_op jit(solution)/shard_map/all_to_all | solution.py:263
  15.0 1.5 %collective-permute-start.1 = (f32[64,2,128]{2,1,0:T(2,128)}, f32[64,2,128]{2,1,0:T(2,128)S(1)}, u32[]{:S(2)}, u32[]{:S(2)}) collective-permute-start(f32[64,2,128]{2,1,0:T(2,128)} %bitcast.23), channel_id=1, source_target_pairs={{0,64},{64,0},{1,65},{65,1},{2,66},{66,2},{3,67},{67,3},{4,68},{68... | collective-permute-start | bytes 196616 | tf_op jit(solution)/shard_map/ppermute | solution.py:261

commit v5 on v4

--- a/solution.py
+++ b/solution.py
@@ -161,7 +161,8 @@
                 bank[pl.ds(target, 1), :] = new
         return carry
 
-    lax.fori_loop(0, senders // group, gather, 0)
+    for step in range(senders // group):
+        gather(step, 0)
 
     lane = lax.broadcasted_iota(jnp.int32, (BLOCK, BLOCK), 1)
     def flush(chunk):

time: 43.9 us -> 43.7 us (level)
  no operation moved by 1% of the time
where the time goes in v5:
time: 43.7 us; the launch traced here: 43.5 us
  waiting for transfers between devices  17.6 us (40%)
  Pallas kernels  12.7 us (29%)
  starting transfers between devices  11.4 us (26%)
  other arithmetic  1.06 us (2%)
  between operations  0.67 us (2%)
    all_to_all x1, waiting for transfers between devices, per_device(): lax.all_to_all(packed.reshape(owners, 1, (slots + 1) * width), ('half', '...  16.1 us
    all_to_all x1, starting transfers between devices, per_device(): lax.all_to_all(packed.reshape(owners, 1, (slots + 1) * width), ('half', '...  11.3 us
    pallas_call x1, Pallas kernels, update(): pl.pallas_call(functools.partial(update_kernel, slots), out_shape=(jax.Sh...  9.75 us
    pallas_call x1, Pallas kernels, pack(): pl.pallas_call(functools.partial(pack_kernel, slots, dead), grid=(steps,)...  2.98 us
    ppermute x1, waiting for transfers between devices, per_device(): got_acc = lax.ppermute(state, 'half', swap)  1.44 us
    select_n x1, other arithmetic, per_device(): jnp.where(bit == 0, mine, theirs)  1 us
  transfers between devices with their start and end apart: 3, of which 2 were waited for; matrix products, arithmetic and copies ran while one was open for 2% of the time, Pallas kernels for 7%

profile of v5, /device:TPU:0, one launch (start us, length us, event | category | flops | bytes accessed | tf_op | source)
XLA Modules:
  0.0 43.5 jit_solution(8099854074533567344)
XLA Ops:
  0.6 0.1 collective-permute-start
  0.7 3.0 %pack.1 = f32[2176,128]{1,0:T(8,128)} custom-call(f32[2048,128]{1,0:T(8,128)} %bitcast.22, s32[16,128]{1,0:T(8,128)} %bitcast.25, s32[1,128]{1,0:T(1,128)} %counts_ref.1), custom_call_target="tpu_custom_call" | custom-call | tf_op jit(solution)/shard_map/pack/pallas_call | solution.py:67
  3.7 11.3 %all-to-all-start = ((f32[128,1,2176]{2,1,0:T(1,128)}), f32[128,1,2176]{2,1,0:T(1,128)S(1)}, u32[]{:S(2)}, u32[]{:S(2)}) async-start(f32[128,1,2176]{2,1,0:T(1,128)} %bitcast.21), calls=%async_computation | async-start | bytes 2228224 | tf_op jit(solution)/shard_map/all_to_all | solution.py:264
  15.0 0.1 collective-permute-start.1
  15.1 1.4 %collective-permute-done.1 = f32[64,2,128]{2,1,0:T(2,128)S(1)} collective-permute-done((f32[64,2,128]{2,1,0:T(2,128)}, f32[64,2,128]{2,1,0:T(2,128)S(1)}, u32[]{:S(2)}, u32[]{:S(2)}) %collective-permute-start.1) | collective-permute-done | bytes 65568 | tf_op jit(solution)/shard_map/ppermute | solution.py:262
  16.5 1.0 %broadcast_select_fusion.1 = (f32[64,1,128]{2,1,0:T(1,128)S(1)}, f32[64,1,128]{2,1,0:T(1,128)S(1)}) fusion(pred[]{:T(512)S(6)} %eq.2, f32[64,2,128]{2,1,0:T(2,128)} %bitcast.24, f32[64,2,128]{2,1,0:T(2,128)S(1)} %collective-permute-done.1), kind=kLoop, calls=%fused_computation.2 | loop fusion | flops 32768 | bytes 196609 | tf_op jit(solution)/shard_map/jit(_where)/select_n | solution.py:273
  17.5 0.1 pad_maximum_fusion
  17.6 16.1 %all-to-all-done = f32[128,1,2176]{2,1,0:T(1,128)S(1)} async-done(((f32[128,1,2176]{2,1,0:T(1,128)}), f32[128,1,2176]{2,1,0:T(1,128)S(1)}, u32[]{:S(2)}, u32[]{:S(2)}) %all-to-all-start) | async-done | bytes 1114144 | tf_op jit(solution)/shard_map/all_to_all | solution.py:264
  33.7 0.0 collective-permute-done.got_ref
  33.7 9.7 %update.1 = (f32[16384,128]{1,0:T(8,128)}, f32[128,128]{1,0:T(8,128)}) custom-call(f32[2,8192,128]{2,1,0:T(8,128)} %bitcast.20, f32[2,8192,128]{2,1,0:T(8,128)} %collective-permute-done.got_ref, f32[128,128]{1,0:T(8,128)S(1)} %bitcast.18, f32[2176,128]{1,0:T(8,128)S(1)} %bitcast.17), custom_call_target="tpu_custom_call" | custom-call | tf_op jit(solution)/shard_map/update/pallas_call | solution.py:229
Async XLA Ops:
  0.6 33.1 %collective-permute-start = (f32[2,8192,128]{2,1,0:T(8,128)}, f32[2,8192,128]{2,1,0:T(8,128)}, u32[]{:S(2)}, u32[]{:S(2)}) collective-permute-start(f32[2,8192,128]{2,1,0:T(8,128)} %bitcast.19), channel_id=1, source_target_pairs={{0,64},{64,0},{1,65},{65,1},{2,66},{66,2},{3,67},{67,3},{4,68},{68... | collective-permute-start | bytes 25165832 | tf_op jit(solution)/shard_map/ppermute | solution.py:261
  3.7 30.0 %all-to-all-start = ((f32[128,1,2176]{2,1,0:T(1,128)}), f32[128,1,2176]{2,1,0:T(1,128)S(1)}, u32[]{:S(2)}, u32[]{:S(2)}) async-start(f32[128,1,2176]{2,1,0:T(1,128)} %bitcast.21), calls=%async_computation | async-start | bytes 2228224 | tf_op jit(solution)/shard_map/all_to_all | solution.py:264
  15.0 1.5 %collective-permute-start.1 = (f32[64,2,128]{2,1,0:T(2,128)}, f32[64,2,128]{2,1,0:T(2,128)S(1)}, u32[]{:S(2)}, u32[]{:S(2)}) collective-permute-start(f32[64,2,128]{2,1,0:T(2,128)} %bitcast.23), channel_id=1, source_target_pairs={{0,64},{64,0},{1,65},{65,1},{2,66},{66,2},{3,67},{67,3},{4,68},{68... | collective-permute-start | bytes 196616 | tf_op jit(solution)/shard_map/ppermute | solution.py:262

commit v6 on v5

--- a/solution.py
+++ b/solution.py
@@ -11,7 +11,7 @@
 EPSILON = 1e-06
 BLOCK = 128
 CHUNK = 1024
-PACK_STEPS = 2
+PACK_STEPS = 4
 
 
 def split(value):
@@ -22,61 +22,93 @@
     return high, middle, low
 
 
-def pack_kernel(slots, dead, grads_ref, ids_ref, counts_ref, out_ref, turned, flat):
+def pack_kernel(
+    slots, dead, grads_ref, ids_hbm, counts_hbm, out_ref, grads, packed, turned, flat, merges, kepts,
+    ids_ref, counts_ref, in_sem, out_sem, ids_sem
+):
     owners = ids_ref.shape[1]
     stride = slots + 1
     group = BLOCK // slots
-    step = pl.program_id(0)
-    batches = grads_ref.shape[0] // BLOCK
-
-    @pl.when(step == 0)
-    def _():
-        slot = lax.broadcasted_iota(jnp.int32, ids_ref.shape, 0)
-        marked = jnp.where(slot < counts_ref[...], ids_ref[...], dead).astype(jnp.float32)
-        filler = jnp.zeros((BLOCK - slots, owners), jnp.float32)
-        turned[...] = jnp.concatenate([marked, filler], 0).T
-        rows = turned[pl.ds(0, owners // group, stride=group), :]
-        for part in range(1, group):
-            piece = turned[pl.ds(part, owners // group, stride=group), :]
-            rows = rows + pltpu.roll(piece, part * slots, 1)
-        flat[...] = rows
+    batches = grads.shape[0] // BLOCK // PACK_STEPS
+    made = batches * group * stride
+
+    def fetch():
+        return pltpu.make_async_copy(grads_ref, grads, in_sem)
+
+    def flush(step):
+        where = pl.ds(step * made, made)
+        return pltpu.make_async_copy(packed.at[where, :], out_ref.at[where, :], out_sem.at[step])
+
+    small = [
+        pltpu.make_async_copy(ids_hbm, ids_ref, ids_sem.at[0]),
+        pltpu.make_async_copy(counts_hbm, counts_ref, ids_sem.at[1]),
+    ]
+    for copy in small:
+        copy.start()
+    fetch().start()
+    for copy in small:
+        copy.wait()
+    slot = lax.broadcasted_iota(jnp.int32, ids_ref.shape, 0)
+    marked = jnp.where(slot < counts_ref[...], ids_ref[...], dead).astype(jnp.float32)
+    filler = jnp.zeros((BLOCK - slots, owners), jnp.float32)
+    turned[...] = jnp.concatenate([marked, filler], 0).T
+    rows = turned[pl.ds(0, owners // group, stride=group), :]
+    for part in range(1, group):
+        piece = turned[pl.ds(part, owners // group, stride=group), :]
+        rows = rows + pltpu.roll(piece, part * slots, 1)
+    flat[...] = rows
 
     below = lax.broadcasted_iota(jnp.int32, (BLOCK, BLOCK), 0)
     across = lax.broadcasted_iota(jnp.int32, (BLOCK, BLOCK), 1)
     together = below // slots == across // slots
     earlier = together & (below < across)
-    for batch in range(batches):
-        row = flat[pl.ds(step * batches + batch, 1), :]
+    for batch in range(batches * PACK_STEPS):
+        row = flat[batch : batch + 1, :]
         wide = jnp.broadcast_to(row, (BLOCK, BLOCK))
         same = wide == wide.T
-        merge = jnp.where(same & together, 1.0, 0.0).astype(jnp.bfloat16)
+        merges[batch * BLOCK : (batch + 1) * BLOCK, :] = jnp.where(
+            same & together, 1.0, 0.0
+        ).astype(jnp.bfloat16)
         seen = jnp.max(jnp.where(same & earlier, 1.0, 0.0), axis=0, keepdims=True)
-        kept = jnp.where(seen > 0, float(dead), row)
+        kepts[batch : batch + 1, :] = jnp.where(seen > 0, float(dead), row)
+    fetch().wait()
+    for batch in range(batches * PACK_STEPS):
+        merge = merges[batch * BLOCK : (batch + 1) * BLOCK, :]
+        kept = kepts[batch : batch + 1, :]
         merged = jnp.zeros((BLOCK, BLOCK), jnp.float32)
-        for part in split(grads_ref[batch * BLOCK : (batch + 1) * BLOCK, :]):
+        for part in split(grads[batch * BLOCK : (batch + 1) * BLOCK, :]):
             merged = merged + jnp.dot(merge, part, preferred_element_type=jnp.float32)
         for owner in range(group):
             base = stride * (batch * group + owner)
-            out_ref[base : base + slots, :] = merged[owner * slots : (owner + 1) * slots, :]
-            out_ref[base + slots : base + stride, :] = kept
+            packed[base : base + slots, :] = merged[owner * slots : (owner + 1) * slots, :]
+            packed[base + slots : base + stride, :] = kept
+        if batch % batches == batches - 1:
+            flush(batch // batches).start()
+    for step in range(PACK_STEPS):
+        flush(step).wait()
 
 
 def pack(grads, ids, counts, dead):
     owners, slots, width = grads.shape
-    steps = PACK_STEPS
+    made = owners * (slots + 1)
+    hbm = pl.BlockSpec(memory_space=pltpu.HBM)
     return pl.pallas_call(
         functools.partial(pack_kernel, slots, dead),
-        grid=(steps,),
-        out_shape=jax.ShapeDtypeStruct((owners * (slots + 1), width), jnp.float32),
-        in_specs=[
-            pl.BlockSpec((owners * slots // steps, width), lambda step: (step, 0)),
-            pl.BlockSpec((slots, owners), lambda step: (0, 0)),
-            pl.BlockSpec((1, owners), lambda step: (0, 0)),
-        ],
-        out_specs=pl.BlockSpec((owners * (slots + 1) // steps, width), lambda step: (step, 0)),
+        out_shape=jax.ShapeDtypeStruct((made, width), jnp.float32),
+        in_specs=[hbm, hbm, hbm],
+        out_specs=hbm,
         scratch_shapes=[
+            pltpu.VMEM((owners * slots, width), jnp.float32),
+            pltpu.VMEM((made, width), jnp.float32),
             pltpu.VMEM((owners, BLOCK), jnp.float32),
             pltpu.VMEM((owners * slots // BLOCK, BLOCK), jnp.float32),
+            pltpu.VMEM((owners * slots, BLOCK), jnp.bfloat16),
+            pltpu.VMEM((owners * slots // BLOCK, BLOCK), jnp.float32),
+            pltpu.VMEM((slots, owners), jnp.int32),
+            pltpu.VMEM((1, owners), jnp.int32),
+            pltpu.SemaphoreType.DMA,
+            pltpu.SemaphoreType.DMA((PACK_STEPS,)),
+            pltpu.SemaphoreType.DMA((2,)),
         ],
         name="pack",
     )(grads.reshape(owners * slots, width), ids.T, counts)

time: 43.7 us -> 43.3 us (level)
  transfers between devices with their start and end apart: 3 -> 3, of which waited for: 2 -> 2; matrix products, arithmetic and copies ran while one was open for 2% -> 2% of each run, Pallas kernels for 7% -> 6%
where the time goes in v6:
time: 43.3 us; the launch traced here: 43.1 us
  waiting for transfers between devices  17.6 us (41%)
  Pallas kernels  12.3 us (28%)
  starting transfers between devices  11.4 us (26%)
  other arithmetic  1.06 us (2%)
  between operations  0.68 us (2%)
    all_to_all x1, waiting for transfers between devices, per_device(): lax.all_to_all(packed.reshape(owners, 1, (slots + 1) * width), ('half', '...  16.1 us
    all_to_all x1, starting transfers between devices, per_device(): lax.all_to_all(packed.reshape(owners, 1, (slots + 1) * width), ('half', '...  11.3 us
    pallas_call x1, Pallas kernels, update(): pl.pallas_call(functools.partial(update_kernel, slots), out_shape=(jax.Sh...  9.72 us
    pallas_call x1, Pallas kernels, pack(): pl.pallas_call(functools.partial(pack_kernel, slots, dead), out_shape=jax...  2.6 us
    ppermute x1, waiting for transfers between devices, per_device(): got_acc = lax.ppermute(state, 'half', swap)  1.44 us
    select_n x1, other arithmetic, per_device(): jnp.where(bit == 0, mine, theirs)  1 us
  transfers between devices with their start and end apart: 3, of which 2 were waited for; matrix products, arithmetic and copies ran while one was open for 2% of the time, Pallas kernels for 6%

profile of v6, /device:TPU:0, one launch (start us, length us, event | category | flops | bytes accessed | tf_op | source)
XLA Modules:
  0.0 43.1 jit_solution(16965131598778534937)
XLA Ops:
  0.6 0.1 collective-permute-start
  0.7 2.6 %pack.1 = f32[2176,128]{1,0:T(8,128)} custom-call(f32[2048,128]{1,0:T(8,128)} %bitcast.22, s32[16,128]{1,0:T(8,128)} %bitcast.25, s32[1,128]{1,0:T(1,128)} %counts_hbm.1), custom_call_target="tpu_custom_call" | custom-call | tf_op jit(solution)/shard_map/pack/pallas_call | solution.py:95
  3.3 11.3 %all-to-all-start = ((f32[128,1,2176]{2,1,0:T(1,128)}), f32[128,1,2176]{2,1,0:T(1,128)S(1)}, u32[]{:S(2)}, u32[]{:S(2)}) async-start(f32[128,1,2176]{2,1,0:T(1,128)} %bitcast.21), calls=%async_computation | async-start | bytes 2228224 | tf_op jit(solution)/shard_map/all_to_all | solution.py:296
  14.6 0.1 collective-permute-start.1
  14.7 1.4 %collective-permute-done.1 = f32[64,2,128]{2,1,0:T(2,128)S(1)} collective-permute-done((f32[64,2,128]{2,1,0:T(2,128)}, f32[64,2,128]{2,1,0:T(2,128)S(1)}, u32[]{:S(2)}, u32[]{:S(2)}) %collective-permute-start.1) | collective-permute-done | bytes 65568 | tf_op jit(solution)/shard_map/ppermute | solution.py:294
  16.2 1.0 %broadcast_select_fusion.1 = (f32[64,1,128]{2,1,0:T(1,128)S(1)}, f32[64,1,128]{2,1,0:T(1,128)S(1)}) fusion(pred[]{:T(512)S(6)} %eq.2, f32[64,2,128]{2,1,0:T(2,128)} %bitcast.24, f32[64,2,128]{2,1,0:T(2,128)S(1)} %collective-permute-done.1), kind=kLoop, calls=%fused_computation.2 | loop fusion | flops 32768 | bytes 196609 | tf_op jit(solution)/shard_map/jit(_where)/select_n | solution.py:305
  17.2 0.1 pad_maximum_fusion
  17.2 16.1 %all-to-all-done = f32[128,1,2176]{2,1,0:T(1,128)S(1)} async-done(((f32[128,1,2176]{2,1,0:T(1,128)}), f32[128,1,2176]{2,1,0:T(1,128)S(1)}, u32[]{:S(2)}, u32[]{:S(2)}) %all-to-all-start) | async-done | bytes 1114144 | tf_op jit(solution)/shard_map/all_to_all | solution.py:296
  33.4 0.0 collective-permute-done.got_ref
  33.4 9.7 %update.1 = (f32[16384,128]{1,0:T(8,128)}, f32[128,128]{1,0:T(8,128)}) custom-call(f32[2,8192,128]{2,1,0:T(8,128)} %bitcast.20, f32[2,8192,128]{2,1,0:T(8,128)} %collective-permute-done.got_ref, f32[128,128]{1,0:T(8,128)S(1)} %bitcast.18, f32[2176,128]{1,0:T(8,128)S(1)} %bitcast.17), custom_call_target="tpu_custom_call" | custom-call | tf_op jit(solution)/shard_map/update/pallas_call | solution.py:261
Async XLA Ops:
  0.6 32.7 %collective-permute-start = (f32[2,8192,128]{2,1,0:T(8,128)}, f32[2,8192,128]{2,1,0:T(8,128)}, u32[]{:S(2)}, u32[]{:S(2)}) collective-permute-start(f32[2,8192,128]{2,1,0:T(8,128)} %bitcast.19), channel_id=1, source_target_pairs={{0,64},{64,0},{1,65},{65,1},{2,66},{66,2},{3,67},{67,3},{4,68},{68... | collective-permute-start | bytes 25165832 | tf_op jit(solution)/shard_map/ppermute | solution.py:293
  3.3 30.0 %all-to-all-start = ((f32[128,1,2176]{2,1,0:T(1,128)}), f32[128,1,2176]{2,1,0:T(1,128)S(1)}, u32[]{:S(2)}, u32[]{:S(2)}) async-start(f32[128,1,2176]{2,1,0:T(1,128)} %bitcast.21), calls=%async_computation | async-start | bytes 2228224 | tf_op jit(solution)/shard_map/all_to_all | solution.py:296
  14.6 1.5 %collective-permute-start.1 = (f32[64,2,128]{2,1,0:T(2,128)}, f32[64,2,128]{2,1,0:T(2,128)S(1)}, u32[]{:S(2)}, u32[]{:S(2)}) collective-permute-start(f32[64,2,128]{2,1,0:T(2,128)} %bitcast.23), channel_id=1, source_target_pairs={{0,64},{64,0},{1,65},{65,1},{2,66},{66,2},{3,67},{67,3},{4,68},{68... | collective-permute-start | bytes 196616 | tf_op jit(solution)/shard_map/ppermute | solution.py:294
